TPU v7x, 256 devices: a whole 4x4x8 slice. The times are simulated.
256 devices in a mesh: row: 8 (over x, z_lo), col: 32 (over y, z_hi, core).
Axes of the slice: x: 4, y: 4, z: 8 (z_hi: 4, z_lo: 2; z = z_hi * 2 + z_lo), core: 2. Of those that a mesh axis runs over, the one named last changes fastest.
Arguments:
- state_cov: float32 [8192, 8192], P('row', 'col'), may hold values from -6 to 6
- trans_first: float32 [64, 9, 128, 128], P('row'), may hold values from -0.1875 to 0.1875
- band_first: int32 [64, 9], P('row'), may hold values from 0 to 63, as said below
- trans_second: float32 [64, 9, 128, 128], P('col'), may hold values from -0.1875 to 0.1875
- band_second: int32 [64, 9], P('col'), may hold values from 0 to 63, as said below
- noise_cov: float32 [8192, 8192], P('col', 'row'), may hold values from -4 to 4
Outputs:
- forecast: float32 [8192, 8192], P('col', 'row')
Inputs may be any that keep to these rules, and one draw needn't show every extreme that they name: `band_first`: row i lists 9 different block columns in increasing order, each within 8 of i; block rows 0 and 63 reach exactly 8 blocks away. `band_second`: row i lists 9 different block columns in increasing order, each within 8 of i; block rows 0 and 63 reach exactly 8 blocks away.
All inputs are finite; a program needn't handle non-finite values.
Results may differ from a plain program's by a relative error of at most 0.0003.
Values sent between devices are 32-bit elements; how exact they have to be, the bound alone decides.
A program may use at most 128 MiB of HBM per device.

v0:
```python
import jax
import jax.numpy as jnp
from jax import lax
from jax.sharding import PartitionSpec as P

BAND = 9
REACH = 8


def extended(block, sides, width):
    for axis, dim in sides:
        count = lax.axis_size(axis)
        forward = [(i, i + 1) for i in range(count - 1)]
        backward = [(target, source) for source, target in forward]
        low = lax.ppermute(
            lax.slice_in_dim(block, block.shape[dim] - width, None, axis=dim), axis, forward
        )
        high = lax.ppermute(lax.slice_in_dim(block, 0, width, axis=dim), axis, backward)
        block = jnp.concatenate([low, block, high], axis=dim)
    return block


def passed_along(x, axis, by):
    length = lax.axis_size(axis)
    pairs = [(i, i + by) for i in range(length) if 0 <= i + by < length]
    return lax.ppermute(x, axis, pairs)


def body(state_cov, trans_first, band_first, trans_second, band_second, noise_cov):
    rows_dev, cols_dev = state_cov.shape
    block_size = trans_first.shape[2]
    band_rows = trans_first.shape[0]
    padded = extended(state_cov, (("row", 0),), REACH * block_size)
    row_base = lax.axis_index("row") * band_rows - REACH
    row_tiles = padded.reshape(-1, block_size, cols_dev)
    picked = jnp.take(row_tiles, (band_first - row_base).reshape(-1), axis=0)
    picked = picked.reshape(band_rows, BAND, block_size, cols_dev)
    advected = jnp.einsum("btxy,btyc->bxc", trans_first, picked, precision=lax.Precision.HIGHEST)
    advected = advected.reshape(rows_dev, cols_dev)
    hop_count = -(-(REACH * block_size) // cols_dev)
    on_left = []
    on_right = []
    for distance in range(1, hop_count + 1):
        on_left.append(passed_along(advected, "col", distance))
        on_right.append(passed_along(advected, "col", -distance))
    widened = jnp.concatenate(on_left[::-1] + [advected] + on_right, axis=1)
    col_blocks = cols_dev // block_size
    col_base = lax.axis_index("col") * col_blocks - hop_count * col_blocks
    strips = widened.reshape(rows_dev, -1, block_size)
    gathered = jnp.take(strips, (band_second - col_base).reshape(-1), axis=1)
    gathered = gathered.reshape(rows_dev, col_blocks, BAND, block_size)
    product = jnp.einsum("jbtk,btik->jbi", gathered, trans_second, precision=lax.Precision.HIGHEST)
    product = product.reshape(rows_dev, cols_dev)
    return product.T + noise_cov


def solution(mesh):
    return jax.shard_map(
        body,
        mesh=mesh,
        in_specs=(
            P("row", "col"),
            P("row", None, None, None),
            P("row", None),
            P("col", None, None, None),
            P("col", None),
            P("col", "row"),
        ),
        out_specs=P("col", "row"),
        check_vma=False,
    )
```

profile of v0, /device:TPU:49, one launch (start us, length us, event | category | flops | bytes accessed | tf_op | source)
XLA Modules:
  0.0 404.2 jit_solution(6295713173958306651)
XLA Ops:
  0.0 2.8 collective-permute-start
  2.8 2.7 collective-permute-start.1
  5.5 0.7 compare_and_fusion
  6.2 0.1 reshape.101
  6.3 20.0 %collective-permute-done = f32[1024,256]{1,0:T(8,128)S(1)} collective-permute-done((f32[1024,256]{1,0:T(8,128)}, f32[1024,256]{1,0:T(8,128)S(1)}, u32[]{:S(2)}, u32[]{:S(2)}) %collective-permute-start) | collective-permute-done | bytes 1048608 | tf_op jit(solution)/shard_map/ppermute | solution.py:15
  26.3 23.4 %collective-permute-done.1 = f32[1024,256]{1,0:T(8,128)S(1)} collective-permute-done((f32[1024,256]{1,0:T(8,128)}, f32[1024,256]{1,0:T(8,128)S(1)}, u32[]{:S(2)}, u32[]{:S(2)}) %collective-permute-start.1) | collective-permute-done | bytes 1048608 | tf_op jit(solution)/shard_map/ppermute | solution.py:18
  49.7 3.1 pad_maximum_fusion
  52.8 9.7 %gather_fusion = f32[72,128,256]{2,1,0:T(8,128)} fusion(f32[24,128,256]{2,1,0:T(8,128)} %bitcast.35, s32[1024]{0:T(1024)S(1)} %pad_clamp_fusion.1), kind=kCustom, calls=%fused_computation | custom fusion | bytes 18874656 | tf_op jit(solution)/shard_map/jit(_take)/gather | solution.py:36
  62.4 9.9 %fusion.2 = f32[8,256,128,1]{1,2,3,0:T(8,128)S(1)} fusion(f32[8,9,128,128]{3,2,1,0:T(8,128)} %param.7, f32[8,9,128,256]{3,2,1,0:T(8,128)} %bitcast.36, pred[8,9]{1,0:T(8,128)(4,1)S(1)} %get-tuple-element.7), kind=kOutput, calls=%fused_computation.4 | convolution fusion | flops 3626237952 | bytes 15204424 | tf_op jit(solution)/shard_map/btxy,btyc->bxc/dot_general | solution.py:38
  72.4 1.3 copy.9
  73.7 7.9 %collective-permute-start.2 = (f32[1024,256]{0,1:T(8,128)}, f32[1024,256]{0,1:T(8,128)}, u32[]{:S(2)}, u32[]{:S(2)}) collective-permute-start(f32[1024,256]{0,1:T(8,128)} %copy.9), channel_id=1, source_target_pairs={{0,4},{1,5},{2,6},{3,7},{4,8},{5,9},{6,10},{7,11},{8,12},{9,13},{1... | collective-permute-start | bytes 3145736 | tf_op jit(solution)/shard_map/ppermute | solution.py:26
  81.6 3.7 collective-permute-start.3
  85.3 4.9 %collective-permute-start.4 = (f32[1024,256]{0,1:T(8,128)}, f32[1024,256]{0,1:T(8,128)}, u32[]{:S(2)}, u32[]{:S(2)}) collective-permute-start(f32[1024,256]{0,1:T(8,128)} %copy.9), channel_id=1, source_target_pairs={{0,2},{1,3},{2,4},{3,5},{4,6},{5,7},{6,8},{7,9},{8,10},{9,11},{10,... | collective-permute-start | bytes 3145736 | tf_op jit(solution)/shard_map/ppermute | solution.py:26
  90.2 1.9 collective-permute-start.5
  92.1 2.4 collective-permute-start.6
  94.5 25.3 %collective-permute-done.2 = f32[1024,256]{0,1:T(8,128)} collective-permute-done((f32[1024,256]{0,1:T(8,128)}, f32[1024,256]{0,1:T(8,128)}, u32[]{:S(2)}, u32[]{:S(2)}) %collective-permute-start.2) | collective-permute-done | bytes 1048608 | tf_op jit(solution)/shard_map/ppermute | solution.py:26
  119.8 17.6 %collective-permute-start.7 = (f32[1024,256]{0,1:T(8,128)}, f32[1024,256]{0,1:T(8,128)}, u32[]{:S(2)}, u32[]{:S(2)}) collective-permute-start(f32[1024,256]{0,1:T(8,128)} %copy.9), channel_id=1, source_target_pairs={{2,0},{3,1},{4,2},{5,3},{6,4},{7,5},{8,6},{9,7},{10,8},{11,9},{12,... | collective-permute-start | bytes 3145736 | tf_op jit(solution)/shard_map/ppermute | solution.py:26
  137.5 140.1 %collective-permute-done.3 = f32[1024,256]{0,1:T(8,128)} collective-permute-done((f32[1024,256]{0,1:T(8,128)}, f32[1024,256]{0,1:T(8,128)}, u32[]{:S(2)}, u32[]{:S(2)}) %collective-permute-start.3) | collective-permute-done | bytes 1048608 | tf_op jit(solution)/shard_map/ppermute | solution.py:26
  277.5 1.9 collective-permute-start.8
  279.5 0.0 collective-permute-done.4
  279.5 7.3 %collective-permute-start.9 = (f32[1024,256]{0,1:T(8,128)}, f32[1024,256]{0,1:T(8,128)}, u32[]{:S(2)}, u32[]{:S(2)}) collective-permute-start(f32[1024,256]{0,1:T(8,128)} %copy.9), channel_id=1, source_target_pairs={{4,0},{5,1},{6,2},{7,3},{8,4},{9,5},{10,6},{11,7},{12,8},{13,9},{1... | collective-permute-start | bytes 3145736 | tf_op jit(solution)/shard_map/ppermute | solution.py:26
  286.8 0.1 reshape.103
  286.9 0.5 concatenate.30
  287.4 2.5 copy.17
  290.0 2.5 copy.18
  292.5 1.5 copy.19
  294.1 13.4 %collective-permute-done.5 = f32[1024,256]{0,1:T(8,128)} collective-permute-done((f32[1024,256]{0,1:T(8,128)}, f32[1024,256]{0,1:T(8,128)}, u32[]{:S(2)}, u32[]{:S(2)}) %collective-permute-start.5) | collective-permute-done | bytes 1048608 | tf_op jit(solution)/shard_map/ppermute | solution.py:26
  307.4 2.6 copy.20
  310.0 0.0 collective-permute-done.6
  310.0 2.5 copy.22
  312.6 0.0 collective-permute-done.7
  312.6 2.6 copy.23
  315.1 2.0 collective-permute-done.8
  317.1 2.5 copy.24
  319.7 2.3 constant_dynamic-update-slice_fusion.7
  322.0 43.3 %collective-permute-done.9 = f32[1024,256]{0,1:T(8,128)} collective-permute-done((f32[1024,256]{0,1:T(8,128)}, f32[1024,256]{0,1:T(8,128)}, u32[]{:S(2)}, u32[]{:S(2)}) %collective-permute-start.9) | collective-permute-done | bytes 1048608 | tf_op jit(solution)/shard_map/ppermute | solution.py:26
  365.3 2.5 copy.25
  367.8 2.4 constant_dynamic-update-slice_fusion.6
  370.3 1.0 constant_dynamic-update-slice_fusion.5
  371.3 2.3 constant_dynamic-update-slice_fusion.4
  373.6 1.0 copy_dynamic-update-slice_fusion
  374.6 2.3 constant_dynamic-update-slice_fusion.3
  377.0 1.1 constant_dynamic-update-slice_fusion.2
  378.0 1.1 constant_dynamic-update-slice_fusion.1
  379.1 1.1 constant_dynamic-update-slice_fusion
  380.2 9.9 %gather_fusion.1 = f32[18,1024,128]{2,1,0:T(8,128)} fusion(f32[1024,18,128]{2,0,1:T(8,128)} %constant_dynamic-update-slice_fusion, s32[1024]{0:T(1024)S(1)} %pad_clamp_fusion), kind=kCustom, calls=%fused_computation.1 | custom fusion | bytes 18874440 | tf_op jit(solution)/shard_map/jit(_take)/gather | solution.py:50
  390.2 12.8 %fusion = f32[2,1024,128,1]{1,2,3,0:T(8,128)S(1)} fusion(f32[2,9,128,128]{3,2,1,0:T(8,128)S(1)} %copy-done, f32[1024,2,9,128]{3,0,2,1:T(8,128)} %bitcast.34, pred[2,9]{1,0:T(4,128)(4,1)S(1)} %get-tuple-element.5), kind=kOutput, calls=%fused_computation.2 | convolution fusion | flops 3626237952 | bytes 11665426 | tf_op jit(solution)/shard_map/jbtk,btik->jbi/dot_general | solution.py:52
  403.0 1.2 bitcast_add_fusion
  (17 shorter events, 0.1 us)
Async XLA Ops:
  0.0 390.2 %copy-start = (f32[2,9,128,128]{3,2,1,0:T(8,128)S(1)}, f32[2,9,128,128]{3,2,1,0:T(8,128)}, u32[]{:S(2)}) copy-start(f32[2,9,128,128]{3,2,1,0:T(8,128)} %param.9) | copy-start | bytes 3538948
  0.0 26.3 %collective-permute-start = (f32[1024,256]{1,0:T(8,128)}, f32[1024,256]{1,0:T(8,128)S(1)}, u32[]{:S(2)}, u32[]{:S(2)}) collective-permute-start(f32[1024,256]{1,0:T(8,128)} %param.6), channel_id=1, source_target_pairs={{0,32},{32,64},{64,96},{96,128},{128,160},{160,192},{192,224},{1,3... | collective-permute-start | bytes 3145736 | tf_op jit(solution)/shard_map/ppermute | solution.py:15
  2.8 46.9 %collective-permute-start.1 = (f32[1024,256]{1,0:T(8,128)}, f32[1024,256]{1,0:T(8,128)S(1)}, u32[]{:S(2)}, u32[]{:S(2)}) collective-permute-start(f32[1024,256]{1,0:T(8,128)} %param.6), channel_id=1, source_target_pairs={{32,0},{64,32},{96,64},{128,96},{160,128},{192,160},{224,192},{33,... | collective-permute-start | bytes 3145736 | tf_op jit(solution)/shard_map/ppermute | solution.py:18
  62.4 224.3 %copy-start.5 = (s32[2,9]{1,0:T(2,128)S(1)}, s32[2,9]{1,0:T(2,128)}, u32[]{:S(2)}) copy-start(s32[2,9]{1,0:T(2,128)} %param.10) | copy-start | bytes 220
  73.7 46.2 %collective-permute-start.2 = (f32[1024,256]{0,1:T(8,128)}, f32[1024,256]{0,1:T(8,128)}, u32[]{:S(2)}, u32[]{:S(2)}) collective-permute-start(f32[1024,256]{0,1:T(8,128)} %copy.9), channel_id=1, source_target_pairs={{0,4},{1,5},{2,6},{3,7},{4,8},{5,9},{6,10},{7,11},{8,12},{9,13},{1... | collective-permute-start | bytes 3145736 | tf_op jit(solution)/shard_map/ppermute | solution.py:26
  81.6 196.0 %collective-permute-start.3 = (f32[1024,256]{0,1:T(8,128)}, f32[1024,256]{0,1:T(8,128)}, u32[]{:S(2)}, u32[]{:S(2)}) collective-permute-start(f32[1024,256]{0,1:T(8,128)} %copy.9), channel_id=1, source_target_pairs={{0,3},{1,4},{2,5},{3,6},{4,7},{5,8},{6,9},{7,10},{8,11},{9,12},{10... | collective-permute-start | bytes 3145736 | tf_op jit(solution)/shard_map/ppermute | solution.py:26
  85.3 194.2 %collective-permute-start.4 = (f32[1024,256]{0,1:T(8,128)}, f32[1024,256]{0,1:T(8,128)}, u32[]{:S(2)}, u32[]{:S(2)}) collective-permute-start(f32[1024,256]{0,1:T(8,128)} %copy.9), channel_id=1, source_target_pairs={{0,2},{1,3},{2,4},{3,5},{4,6},{5,7},{6,8},{7,9},{8,10},{9,11},{10,... | collective-permute-start | bytes 3145736 | tf_op jit(solution)/shard_map/ppermute | solution.py:26
  90.2 217.3 %collective-permute-start.5 = (f32[1024,256]{0,1:T(8,128)}, f32[1024,256]{0,1:T(8,128)}, u32[]{:S(2)}, u32[]{:S(2)}) collective-permute-start(f32[1024,256]{0,1:T(8,128)} %copy.9), channel_id=1, source_target_pairs={{0,1},{1,2},{2,3},{3,4},{4,5},{5,6},{6,7},{7,8},{8,9},{9,10},{10,1... | collective-permute-start | bytes 3145736 | tf_op jit(solution)/shard_map/ppermute | solution.py:26
  92.1 217.9 %collective-permute-start.6 = (f32[1024,256]{0,1:T(8,128)}, f32[1024,256]{0,1:T(8,128)}, u32[]{:S(2)}, u32[]{:S(2)}) collective-permute-start(f32[1024,256]{0,1:T(8,128)} %copy.9), channel_id=1, source_target_pairs={{1,0},{2,1},{3,2},{4,3},{5,4},{6,5},{7,6},{8,7},{9,8},{10,9},{11,1... | collective-permute-start | bytes 3145736 | tf_op jit(solution)/shard_map/ppermute | solution.py:26
  119.8 192.7 %collective-permute-start.7 = (f32[1024,256]{0,1:T(8,128)}, f32[1024,256]{0,1:T(8,128)}, u32[]{:S(2)}, u32[]{:S(2)}) collective-permute-start(f32[1024,256]{0,1:T(8,128)} %copy.9), channel_id=1, source_target_pairs={{2,0},{3,1},{4,2},{5,3},{6,4},{7,5},{8,6},{9,7},{10,8},{11,9},{12,... | collective-permute-start | bytes 3145736 | tf_op jit(solution)/shard_map/ppermute | solution.py:26
  277.5 39.6 %collective-permute-start.8 = (f32[1024,256]{0,1:T(8,128)}, f32[1024,256]{0,1:T(8,128)}, u32[]{:S(2)}, u32[]{:S(2)}) collective-permute-start(f32[1024,256]{0,1:T(8,128)} %copy.9), channel_id=1, source_target_pairs={{3,0},{4,1},{5,2},{6,3},{7,4},{8,5},{9,6},{10,7},{11,8},{12,9},{13... | collective-permute-start | bytes 3145736 | tf_op jit(solution)/shard_map/ppermute | solution.py:26
  279.5 85.8 %collective-permute-start.9 = (f32[1024,256]{0,1:T(8,128)}, f32[1024,256]{0,1:T(8,128)}, u32[]{:S(2)}, u32[]{:S(2)}) collective-permute-start(f32[1024,256]{0,1:T(8,128)} %copy.9), channel_id=1, source_target_pairs={{4,0},{5,1},{6,2},{7,3},{8,4},{9,5},{10,6},{11,7},{12,8},{13,9},{1... | collective-permute-start | bytes 3145736 | tf_op jit(solution)/shard_map/ppermute | solution.py:26
  367.8 9.1 %copy-start.1 = (f32[1024,2,128]{2,0,1:T(8,128)S(1)}, f32[1024,2,128]{2,0,1:T(8,128)}, u32[]{:S(2)}) copy-start(f32[1024,2,128]{2,0,1:T(8,128)} %copy.23) | copy-start | bytes 3145732
  367.8 10.2 %copy-start.2 = (f32[1024,2,128]{2,0,1:T(8,128)S(1)}, f32[1024,2,128]{2,0,1:T(8,128)}, u32[]{:S(2)}) copy-start(f32[1024,2,128]{2,0,1:T(8,128)} %copy.24) | copy-start | bytes 3145732
  367.8 11.3 %copy-start.3 = (f32[1024,2,128]{2,0,1:T(8,128)S(1)}, f32[1024,2,128]{2,0,1:T(8,128)}, u32[]{:S(2)}) copy-start(f32[1024,2,128]{2,0,1:T(8,128)} %copy.25) | copy-start | bytes 3145732
  390.2 12.8 %copy-start.4 = (f32[256,1024]{1,0:T(8,128)S(1)}, f32[256,1024]{1,0:T(8,128)}, u32[]{:S(2)}) copy-start(f32[256,1024]{1,0:T(8,128)} %param.11) | copy-start | bytes 3145732
where the time goes:
time: 405 us; the launch traced here: 404 us
  waiting for transfers between devices  267 us (66%)
  local copies, waits for them, and re-layouts  55.8 us (14%)
  starting transfers between devices  53.1 us (13%)
  matrix products  22.7 us (6%)
  other arithmetic  5 us (1%)
    ppermute x8, waiting for transfers between devices, passed_along(): return lax.ppermute(x, axis, pairs)  224 us
    ppermute x8, starting transfers between devices, passed_along(): return lax.ppermute(x, axis, pairs)  47.6 us
    ppermute x1, waiting for transfers between devices, extended(): lax.ppermute(lax.slice_in_dim(block, 0, width, axis=dim), axis, backward)  23.4 us
    concatenate x10, local copies, waits for them, and re-layouts, body(): widened = jnp.concatenate(on_left[::-1] + [advected] + on_right, axis=1)  21.1 us
    ppermute x1, waiting for transfers between devices, extended(): lax.ppermute(lax.slice_in_dim(block, block.shape[dim] - width, None, axis...  20 us
    unnamed x20, local copies, waits for them, and re-layouts  13.6 us
    dot_general x1, matrix products, body(): jnp.einsum('jbtk,btik->jbi', gathered, trans_second, precision=lax.Precis...  12.8 us
    gather x1, local copies, waits for them, and re-layouts, body(): gathered = jnp.take(strips, (band_second - col_base).reshape(-1), axis=1)  9.94 us
  transfers between devices with their start and end apart: 10, of which 7 were waited for; matrix products, arithmetic and copies ran while one was open for 5% of the time, Pallas kernels for 0%

commit v1 on v0

v1 whole, which is shorter than its diff:
```python
import jax
import jax.numpy as jnp
from jax import lax
from jax.experimental import pallas as pl
from jax.experimental.pallas import tpu as pltpu
from jax.sharding import PartitionSpec as P

BAND = 9
REACH = 8
BS = 128
MESH = pl.DeviceIdType.MESH


def halves(x):
    high = x.astype(jnp.bfloat16)
    low = (x - high.astype(jnp.float32)).astype(jnp.bfloat16)
    return high, low


def dot(a, b):
    return jnp.dot(a, b, preferred_element_type=jnp.float32)


def kernel(
    rows, cols,
    band1, band2, s_ref, a1_ref, a2_ref, out_ref,
    hb, hbh, hbl, a1f, ah, a2f, wh, wl, rx, acc,
    own_send, direct_recv, far_send, far_recv, tile_send, tile_recv, local_sem,
):
    r = lax.axis_index("row")
    c = lax.axis_index("col")
    p = r % 2
    core = c % 2
    mate = r + 1 - 2 * p
    other = c + 1 - 2 * core
    far_to = r + 2 - 4 * p
    far_from = r - 2 + 4 * p
    has_far_to = jnp.logical_and(far_to >= 0, far_to < rows)
    has_far_from = jnp.logical_and(far_from >= 0, far_from < rows)
    left1, right1 = c >= 2, c + 2 < cols
    left2, right2 = c >= 4, c + 4 < cols
    both = jnp.logical_and(left1, right1)
    far_share = jnp.logical_or(
        jnp.logical_and(core == 0, right2), jnp.logical_and(core == 1, left2)
    )

    load_own = pltpu.make_async_copy(s_ref, hb.at[pl.ds(8, 8)], local_sem.at[0])
    load_a1 = pltpu.make_async_copy(a1_ref, a1f, local_sem.at[1])
    load_a2 = pltpu.make_async_copy(a2_ref, a2f, local_sem.at[2])
    load_own.start()
    load_a2.start()
    load_a1.start()

    barrier = pltpu.get_barrier_semaphore()
    neighbours = (
        (None, (mate, c)),
        (None, (r, other)),
        (left1, (r, c - 2)),
        (right1, (r, c + 2)),
        (r >= 2, (r - 2, c)),
        (r + 2 < rows, (r + 2, c)),
    )
    for cond, device in neighbours:
        def greet(device=device):
            pl.semaphore_signal(barrier, inc=1, device_id=device, device_id_type=MESH)
        greet() if cond is None else pl.when(cond)(greet)
    peers = jnp.int32(0)
    for cond, _ in neighbours:
        peers = peers + (1 if cond is None else cond.astype(jnp.int32))
    pl.semaphore_wait(barrier, peers)

    def remote(src, dst, send, recv, device):
        return pltpu.make_async_remote_copy(
            src_ref=src, dst_ref=dst, send_sem=send, recv_sem=recv,
            device_id=device, device_id_type=MESH,
        )

    near_at = 16 - 16 * p
    away_at = 16 * p

    def send_own(k):
        return remote(s_ref.at[k], hb.at[16 * p + k], own_send.at[k], direct_recv.at[k], (mate, c))

    def got_direct(k):
        return remote(s_ref.at[k], hb.at[near_at + k], own_send.at[k], direct_recv.at[k], (mate, c))

    def send_far(k):
        return remote(hb.at[near_at + k], hb.at[16 * p + k], far_send.at[k], far_recv.at[k], (far_to, c))

    def got_far(k):
        return remote(hb.at[near_at + k], hb.at[away_at + k], far_send.at[k], far_recv.at[k], (mate, c))

    def each(n, body):
        def step(k, carry):
            body(k)
            return carry
        lax.fori_loop(0, n, step, 0)

    each(8, lambda k: send_own(k).start())
    load_own.wait()
    load_a2.wait()
    load_a1.wait()

    def build_w(d):
        for j in range(2):
            for kk in range(2):
                block = 2 * c - REACH + 2 * d + kk
                slot = jnp.int32(0)
                there = jnp.int32(0)
                for t in range(BAND):
                    hit = (band2[j, t] == block).astype(jnp.int32)
                    slot = slot + t * hit
                    there = there + hit
                m = (a2f[j, jnp.minimum(slot, BAND - 1)] * there.astype(jnp.float32)).T
                h, l = halves(m)
                wh[d, kk * BS:(kk + 1) * BS, j * BS:(j + 1) * BS] = h
                wl[d, kk * BS:(kk + 1) * BS, j * BS:(j + 1) * BS] = l

    def split_rows(at):
        h, l = halves(hb[at])
        hbh[at] = h
        hbl[at] = l

    def halo_step(k):
        for t in range(BAND):
            h, l = halves(a1f[k, t])
            ah[k, 0:BS, t * BS:(t + 1) * BS] = h
            ah[k, BS:2 * BS, t * BS:(t + 1) * BS] = l
        build_w(k)
        split_rows(8 + k)
        got_direct(k).wait_recv()

        @pl.when(has_far_to)
        def _():
            send_far(k).start()

        split_rows(near_at + k)

    each(8, halo_step)
    build_w(8)

    @pl.when(has_far_from)
    def _():
        def step(k):
            got_far(k).wait_recv()
            split_rows(away_at + k)
        each(8, step)

    RIGHT, LEFT, SHARE, FWD_RIGHT, FWD_LEFT, SHARE_L, SHARE_R, SHARE_FAR = range(8)

    def tile_copy(kind, i):
        src, dst, device = {
            RIGHT: (4, 2, (r, c + 2)),
            LEFT: (4, 6, (r, c - 2)),
            SHARE: (4, 3 + 2 * core, (r, other)),
            FWD_RIGHT: (2, 0, (r, c + 2)),
            FWD_LEFT: (6, 8, (r, c - 2)),
            SHARE_L: (2, 1 + 2 * core, (r, other)),
            SHARE_R: (6, 5 + 2 * core, (r, other)),
            SHARE_FAR: (8 - 8 * core, 7 - 6 * core, (r, other)),
        }[kind]
        return remote(rx.at[src, i], rx.at[dst, i], tile_send.at[kind, i], tile_recv.at[dst, i], device)

    def got_tile(slot, i):
        return remote(rx.at[4, i], rx.at[slot, i], tile_send.at[0, i], tile_recv.at[slot, i], (r, other))

    def add_tile(slot, i, first=False):
        h, l = halves(rx[slot, i])
        top = dot(jnp.concatenate([h, l], axis=0), wh[slot])
        total = top[:BS] + top[BS:] + dot(h, wl[slot])
        if first:
            acc[i] = total
        else:
            acc[i] += total

    def advect(i):
        ids = [jnp.clip(band1[i, t] - 8 * r + REACH, 0, 23) for t in range(BAND)]
        xh = jnp.concatenate([hbh[k] for k in ids], axis=0)
        xl = jnp.concatenate([hbl[k] for k in ids], axis=0)
        top = dot(ah[i], xh)
        rx[4, i] = top[:BS] + top[BS:] + dot(ah[i, 0:BS], xl)

        @pl.when(right1)
        def _():
            tile_copy(RIGHT, i).start()

        @pl.when(left1)
        def _():
            tile_copy(LEFT, i).start()

        tile_copy(SHARE, i).start()

    each(8, advect)

    each(8, lambda i: add_tile(4, i, first=True))

    def near_step(i):
        got_tile(5 - 2 * core, i).wait_recv()
        add_tile(5 - 2 * core, i)

        @pl.when(left1)
        def _():
            got_tile(2, i).wait_recv()
            tile_copy(SHARE_L, i).start()

            @pl.when(right1)
            def _():
                tile_copy(FWD_RIGHT, i).start()

            add_tile(2, i)

        @pl.when(right1)
        def _():
            got_tile(6, i).wait_recv()
            tile_copy(SHARE_R, i).start()

            @pl.when(left1)
            def _():
                tile_copy(FWD_LEFT, i).start()

            add_tile(6, i)

    each(8, near_step)

    def mid_step(i):
        @pl.when(left1)
        def _():
            got_tile(3 - 2 * core, i).wait_recv()
            add_tile(3 - 2 * core, i)

        @pl.when(right1)
        def _():
            got_tile(7 - 2 * core, i).wait_recv()
            add_tile(7 - 2 * core, i)

    each(8, mid_step)

    def far_step(i):
        @pl.when(left2)
        def _():
            got_tile(0, i).wait_recv()

        @pl.when(right2)
        def _():
            got_tile(8, i).wait_recv()

        @pl.when(far_share)
        def _():
            tile_copy(SHARE_FAR, i).start()

        @pl.when(left2)
        def _():
            add_tile(0, i)

        @pl.when(right2)
        def _():
            add_tile(8, i)

        @pl.when(jnp.logical_or(
            jnp.logical_and(core == 0, left2), jnp.logical_and(core == 1, right2)
        ))
        def _():
            got_tile(1 + 6 * core, i).wait_recv()
            add_tile(1 + 6 * core, i)

        out_ref[:, pl.ds(pl.multiple_of(i * BS, BS), BS)] = acc[i].T

    each(8, far_step)

    def drain(i):
        send_own(i).wait_send()
        tile_copy(SHARE, i).wait_send()

        @pl.when(has_far_to)
        def _():
            send_far(i).wait_send()

        @pl.when(right1)
        def _():
            tile_copy(RIGHT, i).wait_send()
            tile_copy(SHARE_R, i).wait_send()

        @pl.when(left1)
        def _():
            tile_copy(LEFT, i).wait_send()
            tile_copy(SHARE_L, i).wait_send()

        @pl.when(both)
        def _():
            tile_copy(FWD_RIGHT, i).wait_send()
            tile_copy(FWD_LEFT, i).wait_send()

        @pl.when(far_share)
        def _():
            tile_copy(SHARE_FAR, i).wait_send()

    each(8, drain)


def solution(mesh):
    rows, cols = mesh.shape["row"], mesh.shape["col"]

    def body(state_cov, trans_first, band_first, trans_second, band_second, noise_cov):
        width = state_cov.shape[1]
        tiles = state_cov.reshape(8, BS, width)
        f32, bf16 = jnp.float32, jnp.bfloat16
        smem = pl.BlockSpec(memory_space=pltpu.SMEM)
        anyspace = pl.BlockSpec(memory_space=pl.ANY)
        product = pl.pallas_call(
            lambda *refs: kernel(rows, cols, *refs),
            out_shape=jax.ShapeDtypeStruct((width, 8 * BS), f32),
            in_specs=[smem, smem, anyspace, anyspace, anyspace],
            out_specs=pl.BlockSpec(memory_space=pltpu.VMEM),
            scratch_shapes=[
                pltpu.VMEM((24, BS, width), f32),
                pltpu.VMEM((24, BS, width), bf16),
                pltpu.VMEM((24, BS, width), bf16),
                pltpu.VMEM((8, BAND, BS, BS), f32),
                pltpu.VMEM((8, 2 * BS, BAND * BS), bf16),
                pltpu.VMEM((2, BAND, BS, BS), f32),
                pltpu.VMEM((9, width, width), bf16),
                pltpu.VMEM((9, width, width), bf16),
                pltpu.VMEM((9, 8, BS, width), f32),
                pltpu.VMEM((8, BS, width), f32),
                pltpu.SemaphoreType.DMA((8,)),
                pltpu.SemaphoreType.DMA((8,)),
                pltpu.SemaphoreType.DMA((8,)),
                pltpu.SemaphoreType.DMA((8,)),
                pltpu.SemaphoreType.DMA((8, 8)),
                pltpu.SemaphoreType.DMA((9, 8)),
                pltpu.SemaphoreType.DMA((3,)),
            ],
            compiler_params=pltpu.CompilerParams(
                collective_id=0, has_side_effects=True, vmem_limit_bytes=60 * 2**20
            ),
            name="forecast",
        )(band_first, band_second, tiles, trans_first, trans_second)
        return product + noise_cov

    return jax.shard_map(
        body,
        mesh=mesh,
        in_specs=(
            P("row", "col"),
            P("row", None, None, None),
            P("row", None),
            P("col", None, None, None),
            P("col", None),
            P("col", "row"),
        ),
        out_specs=P("col", "row"),
        check_vma=False,
    )
```

time: 405 us -> 141 us (0.35)
  the two profiles are of different devices: /device:TPU:49 before, /device:TPU:37 now
where the time goes in v1:
time: 141 us
  Pallas kernels  138 us (98%)
  other arithmetic  2.38 us (2%)
    pallas_call x1, Pallas kernels, body(): pl.pallas_call(lambda *refs: kernel(rows, cols, *refs), out_shape=jax.Sha...  138 us

profile of v1, /device:TPU:37, one launch (start us, length us, event | category | flops | bytes accessed | tf_op | source)
XLA Modules:
  0.0 140.8 jit_solution(11678702050652452224)
XLA Ops:
  0.0 0.0 copy-start
  0.0 138.4 %forecast.1 = f32[256,1024]{1,0:T(8,128)} custom-call(s32[8,9]{1,0:T(8,128)} %refs_0_.1, s32[2,9]{1,0:T(2,128)} %refs_1_.1, f32[8,128,256]{2,1,0:T(8,128)} %bitcast.1, f32[8,9,128,128]{3,2,1,0:T(8,128)} %refs_3_.1, f32[2,9,128,128]{3,2,1,0:T(8,128)} %refs_4_.1), custom_call_target="tpu_custom_call" | custom-call | tf_op jit(solution)/shard_map/forecast/pallas_call | solution.py:309
  138.4 0.0 copy-done
  138.4 2.4 %add.3 = f32[256,1024]{1,0:T(8,128)} add(f32[256,1024]{1,0:T(8,128)} %forecast.1, f32[256,1024]{1,0:T(8,128)S(1)} %copy-done) | non-fusion elementwise | flops 262144 | bytes 3145728 | tf_op jit(solution)/shard_map/add | solution.py:338
Async XLA Ops:
  0.0 138.4 %copy-start = (f32[256,1024]{1,0:T(8,128)S(1)}, f32[256,1024]{1,0:T(8,128)}, u32[]{:S(2)}) copy-start(f32[256,1024]{1,0:T(8,128)} %param.11) | copy-start | bytes 3145732

commit v2 on v0

v2 whole, which is shorter than its diff:
```python
import jax
import jax.numpy as jnp
from jax import lax
from jax.experimental import pallas as pl
from jax.experimental.pallas import tpu as pltpu
from jax.sharding import PartitionSpec as P

BAND = 9
REACH = 8
BS = 128
MESH = pl.DeviceIdType.MESH


def halves(x):
    high = x.astype(jnp.bfloat16)
    low = (x - high.astype(jnp.float32)).astype(jnp.bfloat16)
    return high, low


def dot(a, b):
    return jnp.dot(a, b, preferred_element_type=jnp.float32)


def product(a, xs_high, xs_low):
    top = dot(a, jnp.concatenate(xs_high, axis=0))
    return top[:BS] + top[BS:] + dot(a[:BS], jnp.concatenate(xs_low, axis=0))


def each(n, body):
    def step(k, carry):
        body(k)
        return carry
    lax.fori_loop(0, n, step, 0)


def remote(src, dst, send, recv, device):
    return pltpu.make_async_remote_copy(
        src_ref=src, dst_ref=dst, send_sem=send, recv_sem=recv,
        device_id=device, device_id_type=MESH,
    )


def both(*conds):
    out = conds[0]
    for cond in conds[1:]:
        out = jnp.logical_and(out, cond)
    return out


def either(*conds):
    out = conds[0]
    for cond in conds[1:]:
        out = jnp.logical_or(out, cond)
    return out


def kernel(
    rows, cols,
    band1, band2, s_ref, a1_ref, a2_ref, out_ref,
    hb, hbh, hbl, a1f, a1s, a2f, a2s, stage, g0, g1, gh, gl, res, resin, band_mine, band_all, bands,
    own_send, direct_recv, far_send, far_recv,
    slab_send, slab_recv, chain_send, wide_send, wide_recv,
    band_send, band_recv, in_send, in_recv, share_send, share_recv, side_send, side_recv,
    back_send, back_recv, local_sem,
):
    r = lax.axis_index("row")
    c = lax.axis_index("col")
    y = c // 8
    q = c % 8
    h = q // 2
    core = q % 2
    owner = h // 2
    mine = q % 4
    base = 8 * y + 4 * core
    local_owner = core == owner
    x = r // 2
    p = r % 2
    mate = r + 1 - 2 * p
    other = c + 1 - 2 * core
    far_to = r + 2 - 4 * p
    far_from = r - 2 + 4 * p
    has_far_to = both(far_to >= 0, far_to < rows)
    has_far_from = both(far_from >= 0, far_from < rows)
    side = c - 7 + 14 * core
    has_side = both(side >= 0, side < cols)
    out_row = r + 1 - 2 * p
    out_h = (h + 3 + 2 * p) % 4

    load_own = pltpu.make_async_copy(s_ref, hb.at[pl.ds(8, 8)], local_sem.at[0])
    load_a1 = pltpu.make_async_copy(a1_ref, a1f, local_sem.at[1])
    load_a2 = pltpu.make_async_copy(a2_ref, a2f.at[mine], local_sem.at[2])
    load_own.start()
    load_a1.start()

    @pl.when(local_owner)
    def _():
        load_a2.start()

    barrier = pltpu.get_barrier_semaphore()

    def greet(device):
        pl.semaphore_signal(barrier, inc=1, device_id=device, device_id_type=MESH)

    for o in range(1, 8):
        greet((r, 8 * y + (q + o) % 8))
    for o in range(1, rows // 2):
        greet(((r + 2 * o) % rows, c))
    for k in range(2):
        greet((mate, 8 * y + 2 * h + k))
        greet((out_row, 8 * y + 2 * out_h + k))

    @pl.when(has_side)
    def _():
        greet((r, side))

    pl.semaphore_wait(barrier, 7 + rows // 2 - 1 + 4 + has_side.astype(jnp.int32))

    near_at = 16 - 16 * p
    away_at = 16 * p

    def send_own(k):
        return remote(s_ref.at[k], hb.at[16 * p + k], own_send.at[k], direct_recv.at[k], (mate, c))

    def got_direct(k):
        return remote(s_ref.at[k], hb.at[near_at + k], own_send.at[k], direct_recv.at[k], (mate, c))

    def send_far(k):
        return remote(hb.at[near_at + k], hb.at[16 * p + k], far_send.at[k], far_recv.at[k], (far_to, c))

    def got_far(k):
        return remote(hb.at[near_at + k], hb.at[away_at + k], far_send.at[k], far_recv.at[k], (mate, c))

    each(8, lambda k: send_own(k).start())

    part = BS // (rows // 2)

    def piece(m, at):
        return a2f.at[m, :, :, pl.ds(pl.multiple_of(part * at, part), part), :]

    slab_to_mate_core = remote(a2_ref, a2f.at[mine], slab_send.at[0], slab_recv.at[mine], (r, other))
    slab_out = remote(
        a2_ref.at[:, :, pl.ds(pl.multiple_of(part * x, part), part), :], piece(mine, x),
        slab_send.at[1], slab_recv.at[mine], (out_row, 8 * y + 2 * out_h + owner),
    )
    slab_out.start()

    @pl.when(jnp.logical_not(local_owner))
    def _():
        slab_to_mate_core.start()

    def far_of(m):
        return (2 * core + m // 2 - h + 4) % 4

    def chain_conds(m):
        d = far_of(m)
        first = m % 2 == 0
        to_mate = either(
            both(d == 3, p == 0), both(d == 1, p == 1),
            both(d == 2, first, p == 0), both(d == 2, jnp.logical_not(first), p == 1),
        )
        to_out = either(both(d == 3, p == 1, first), both(d == 1, p == 0, jnp.logical_not(first)))
        return d, to_mate, to_out

    def chain_copy(m, way):
        device = (mate, c) if way == 0 else (out_row, 8 * y + 2 * out_h + core)
        return remote(piece(m, x), piece(m, x), chain_send.at[m, way], slab_recv.at[m], device)

    def wide_copy(m, o):
        return remote(piece(m, x), piece(m, x), wide_send.at[m, o - 1], wide_recv.at[m, o - 1], ((r + 2 * o) % rows, c))

    def got_wide(m, o):
        at = (x - o + rows // 2) % (rows // 2)
        return remote(piece(m, x), piece(m, at), wide_send.at[m, o - 1], wide_recv.at[m, o - 1], (mate, c))

    def chain_step(m, far):
        d, to_mate, to_out = chain_conds(m)

        @pl.when((d == 2) if far else (d % 2 == 1))
        def _():
            chain_copy(m, 0).wait_recv()

            @pl.when(to_mate)
            def _():
                chain_copy(m, 0).start()

            @pl.when(to_out)
            def _():
                chain_copy(m, 1).start()

            for o in range(1, rows // 2):
                wide_copy(m, o).start()

    row_id = lax.broadcasted_iota(jnp.int32, (8, BS), 0)
    lane_id = lax.broadcasted_iota(jnp.int32, (8, BS), 1)
    table = jnp.zeros((8, BS), jnp.int32)
    for j in range(2):
        for t in range(BAND):
            table = jnp.where(both(row_id == j, lane_id == t), band2[j, t], table)
    band_mine[...] = table

    @pl.when(local_owner)
    def _():
        band_all[mine] = table

    def group_copy(src, dst, send, recv, o):
        return remote(src, dst, send, recv, (r, 8 * y + 2 * ((h + o) % 4) + owner))

    def band_copy(o):
        return group_copy(band_mine, band_all.at[mine], band_send.at[o], band_recv.at[mine], o)

    def got_band(m):
        return remote(band_mine, band_all.at[m], band_send.at[0], band_recv.at[m], (mate, c))

    def is_remote(o):
        return jnp.logical_or(o != 0, jnp.logical_not(local_owner))

    for o in range(4):
        @pl.when(is_remote(o))
        def _():
            band_copy(o).start()

    load_own.wait()
    load_a1.wait()

    def split_rows(at):
        high, low = halves(hb[at])
        hbh[at] = high
        hbl[at] = low

    def halo_step(k):
        for t in range(BAND):
            high, low = halves(a1f[k, t])
            a1s[k, 0:BS, t * BS:(t + 1) * BS] = high
            a1s[k, BS:2 * BS, t * BS:(t + 1) * BS] = low
        split_rows(8 + k)
        got_direct(k).wait_recv()

        @pl.when(has_far_to)
        def _():
            send_far(k).start()

        split_rows(near_at + k)

    each(4, halo_step)
    each(4, lambda m: chain_step(m, False))
    each(4, lambda k: halo_step(4 + k))
    each(4, lambda m: chain_step(m, True))

    @pl.when(has_far_from)
    def _():
        def step(k):
            got_far(k).wait_recv()
            split_rows(away_at + k)
        each(8, step)

    gs = (g0, g1)

    def in_copy(e, o):
        hp = (h + o) % 4
        return group_copy(stage.at[e, hp], gs[e].at[pl.ds(8 + 2 * mine, 2)], in_send.at[e, o], in_recv.at[e, mine], o)

    def got_in(e, m):
        return remote(stage.at[e, 0], gs[e].at[pl.ds(8 + 2 * m, 2)], in_send.at[e, 0], in_recv.at[e, m], (mate, c))

    for e in range(2):
        def advect(n, e=e):
            o = 3 - n
            hp = (h + o) % 4
            i = 2 * hp + e
            ids = [jnp.clip(band1[i, t] - 8 * r + REACH, 0, 23) for t in range(BAND)]
            tile = product(a1s[i], [hbh[k] for k in ids], [hbl[k] for k in ids])
            for b in range(2):
                stage[e, hp, b] = tile[:, b * BS:(b + 1) * BS].T

            @pl.when(is_remote(o))
            def _():
                in_copy(e, o).start()

            @pl.when(jnp.logical_not(is_remote(o)))
            def _():
                for b in range(2):
                    gs[e][8 + 2 * mine + b] = stage[e, hp, b]
        each(4, advect)

    for m in range(4):
        @pl.when(base + m != c)
        def _():
            got_band(m).wait_recv()
    to_scalars = pltpu.make_async_copy(band_all, bands, local_sem.at[3])
    to_scalars.start()

    def share_copy(e, m):
        return remote(
            gs[e].at[pl.ds(8 + 2 * m, 2)], gs[e].at[pl.ds(16 * core + 2 * m, 2)],
            share_send.at[e, m], share_recv.at[e, m], (r, other),
        )

    def side_copy(e, m):
        return remote(
            gs[e].at[pl.ds(8 + 2 * m, 2)], gs[e].at[pl.ds(16 - 16 * core + 2 * m, 2)],
            side_send.at[e, m], side_recv.at[e, m], (r, side),
        )

    def got_share(e, m):
        return remote(
            gs[e].at[pl.ds(8 + 2 * m, 2)], gs[e].at[pl.ds(16 - 16 * core + 2 * m, 2)],
            share_send.at[e, m], share_recv.at[e, m], (r, other),
        )

    def got_side(e, m):
        return remote(
            gs[e].at[pl.ds(8 + 2 * m, 2)], gs[e].at[pl.ds(16 * core + 2 * m, 2)],
            side_send.at[e, m], side_recv.at[e, m], (r, other),
        )

    def back_copy(e, m):
        return remote(res.at[e, m], resin.at[e, h], back_send.at[e, m], back_recv.at[e, h], (r, base + m))

    def got_back(e, hp):
        return remote(res.at[e, 0], resin.at[e, hp], back_send.at[e, 0], back_recv.at[e, hp], (mate, c))

    def split_pair(g, at):
        for b in range(2):
            high, low = halves(g[at + b])
            gh[at + b] = high
            gl[at + b] = low

    for e in range(2):
        def own_step(m, e=e):
            @pl.when(base + m != c)
            def _():
                got_in(e, m).wait_recv()

            share_copy(e, m).start()

            @pl.when(has_side)
            def _():
                side_copy(e, m).start()

            split_pair(gs[e], 8 + 2 * m)

        each(4, own_step)

        if e == 0:
            to_scalars.wait()

            @pl.when(local_owner)
            def _():
                load_a2.wait()

            def slab_step(m):
                @pl.when(both(far_of(m) == 0, base + m != c))
                def _():
                    remote(a2_ref, a2f.at[m], slab_send.at[0], slab_recv.at[m], (r, other)).wait_recv()

                @pl.when(far_of(m) != 0)
                def _():
                    for o in range(1, rows // 2):
                        got_wide(m, o).wait_recv()

                for jj in range(2):
                    for t in range(BAND):
                        high, low = halves(a2f[m, jj, t])
                        a2s[2 * m + jj, 0:BS, t * BS:(t + 1) * BS] = high
                        a2s[2 * m + jj, BS:2 * BS, t * BS:(t + 1) * BS] = low

            each(4, slab_step)

        def neighbour_step(m, e=e):
            got_share(e, m).wait_recv()
            split_pair(gs[e], 16 - 16 * core + 2 * m)

            @pl.when(has_side)
            def _():
                got_side(e, m).wait_recv()
                split_pair(gs[e], 16 * core + 2 * m)

        each(4, neighbour_step)

        def second(m, e=e):
            for jj in range(2):
                ids = [jnp.clip(bands[m, jj, t] - 2 * base + REACH, 0, 23) for t in range(BAND)]
                res[e, m, jj] = product(a2s[2 * m + jj], [gh[k] for k in ids], [gl[k] for k in ids])

            @pl.when(base + m != c)
            def _():
                back_copy(e, m).start()

        each(4, second)

    for e in range(2):
        def finish(hp, e=e):
            columns = pl.ds(pl.multiple_of((2 * hp + e) * BS, BS), BS)
            here = both(hp == h, local_owner)

            @pl.when(jnp.logical_not(here))
            def _():
                got_back(e, hp).wait_recv()
                for jj in range(2):
                    out_ref[jj * BS:(jj + 1) * BS, columns] = resin[e, hp, jj]

            @pl.when(here)
            def _():
                for jj in range(2):
                    out_ref[jj * BS:(jj + 1) * BS, columns] = res[e, mine, jj]

        each(4, finish)

    slab_out.wait_send()

    @pl.when(jnp.logical_not(local_owner))
    def _():
        slab_to_mate_core.wait_send()

    def drain_halo(k):
        send_own(k).wait_send()

        @pl.when(has_far_to)
        def _():
            send_far(k).wait_send()

    each(8, drain_halo)

    def drain(m):
        d, to_mate, to_out = chain_conds(m)

        @pl.when(d != 0)
        def _():
            @pl.when(to_mate)
            def _():
                chain_copy(m, 0).wait_send()

            @pl.when(to_out)
            def _():
                chain_copy(m, 1).wait_send()

            for o in range(1, rows // 2):
                wide_copy(m, o).wait_send()

        @pl.when(is_remote(m))
        def _():
            band_copy(m).wait_send()
            for e in range(2):
                in_copy(e, m).wait_send()

        for e in range(2):
            share_copy(e, m).wait_send()

            @pl.when(has_side)
            def _():
                side_copy(e, m).wait_send()

            @pl.when(base + m != c)
            def _():
                back_copy(e, m).wait_send()

    each(4, drain)


def solution(mesh):
    rows, cols = mesh.shape["row"], mesh.shape["col"]

    def body(state_cov, trans_first, band_first, trans_second, band_second, noise_cov):
        width = state_cov.shape[1]
        tiles = state_cov.reshape(8, BS, width)
        f32, bf16, i32 = jnp.float32, jnp.bfloat16, jnp.int32
        smem = pl.BlockSpec(memory_space=pltpu.SMEM)
        anyspace = pl.BlockSpec(memory_space=pl.ANY)
        dma = pltpu.SemaphoreType.DMA
        product_t = pl.pallas_call(
            lambda *refs: kernel(rows, cols, *refs),
            out_shape=jax.ShapeDtypeStruct((width, 8 * BS), f32),
            in_specs=[smem, smem, anyspace, anyspace, anyspace],
            out_specs=pl.BlockSpec(memory_space=pltpu.VMEM),
            scratch_shapes=[
                pltpu.VMEM((24, BS, width), f32),
                pltpu.VMEM((24, BS, width), bf16),
                pltpu.VMEM((24, BS, width), bf16),
                pltpu.VMEM((8, BAND, BS, BS), f32),
                pltpu.VMEM((8, 2 * BS, BAND * BS), bf16),
                pltpu.VMEM((4, 2, BAND, BS, BS), f32),
                pltpu.VMEM((8, 2 * BS, BAND * BS), bf16),
                pltpu.VMEM((2, 4, 2, BS, BS), f32),
                pltpu.VMEM((24, BS, BS), f32),
                pltpu.VMEM((24, BS, BS), f32),
                pltpu.VMEM((24, BS, BS), bf16),
                pltpu.VMEM((24, BS, BS), bf16),
                pltpu.VMEM((2, 4, 2, BS, BS), f32),
                pltpu.VMEM((2, 4, 2, BS, BS), f32),
                pltpu.VMEM((8, BS), i32),
                pltpu.VMEM((4, 8, BS), i32),
                pltpu.SMEM((4, 8, BS), i32),
                dma((8,)), dma((8,)), dma((8,)), dma((8,)),
                dma((2,)), dma((4,)), dma((4, 2)), dma((4, 3)), dma((4, 3)),
                dma((4,)), dma((4,)), dma((2, 4)), dma((2, 4)),
                dma((2, 4)), dma((2, 4)), dma((2, 4)), dma((2, 4)),
                dma((2, 4)), dma((2, 4)), dma((4,)),
            ],
            compiler_params=pltpu.CompilerParams(
                collective_id=0, has_side_effects=True, vmem_limit_bytes=60 * 2**20
            ),
            name="forecast",
        )(band_first, band_second, tiles, trans_first, trans_second)
        return product_t + noise_cov

    return jax.shard_map(
        body,
        mesh=mesh,
        in_specs=(
            P("row", "col"),
            P("row", None, None, None),
            P("row", None),
            P("col", None, None, None),
            P("col", None),
            P("col", "row"),
        ),
        out_specs=P("col", "row"),
        check_vma=False,
    )
```

time: 405 us -> 128 us (0.32)
  the two profiles are of different devices: /device:TPU:49 before, /device:TPU:95 now
where the time goes in v2:
time: 128 us
  Pallas kernels  126 us (98%)
  other arithmetic  2.38 us (2%)
    pallas_call x1, Pallas kernels, body(): pl.pallas_call(lambda *refs: kernel(rows, cols, *refs), out_shape=jax.Sha...  126 us

profile of v2, /device:TPU:95, one launch (start us, length us, event | category | flops | bytes accessed | tf_op | source)
XLA Modules:
  0.0 128.3 jit_solution(16798256625549705324)
XLA Ops:
  0.0 0.0 copy-start
  0.0 125.9 %forecast.1 = f32[256,1024]{1,0:T(8,128)} custom-call(s32[8,9]{1,0:T(8,128)} %refs_0_.1, s32[2,9]{1,0:T(2,128)} %refs_1_.1, f32[8,128,256]{2,1,0:T(8,128)} %bitcast.1, f32[8,9,128,128]{3,2,1,0:T(8,128)} %refs_3_.1, f32[2,9,128,128]{3,2,1,0:T(8,128)} %refs_4_.1), custom_call_target="tpu_custom_call" | custom-call | tf_op jit(solution)/shard_map/forecast/pallas_call | solution.py:470
  125.9 0.0 copy-done
  125.9 2.4 %add.3 = f32[256,1024]{1,0:T(8,128)} add(f32[256,1024]{1,0:T(8,128)} %forecast.1, f32[256,1024]{1,0:T(8,128)S(1)} %copy-done) | non-fusion elementwise | flops 262144 | bytes 3145728 | tf_op jit(solution)/shard_map/add | solution.py:504
Async XLA Ops:
  0.0 125.9 %copy-start = (f32[256,1024]{1,0:T(8,128)S(1)}, f32[256,1024]{1,0:T(8,128)}, u32[]{:S(2)}) copy-start(f32[256,1024]{1,0:T(8,128)} %param.11) | copy-start | bytes 3145732

commit v3 on v2

--- a/solution.py
+++ b/solution.py
@@ -153,17 +153,13 @@
 
     def chain_conds(m):
         d = far_of(m)
-        first = m % 2 == 0
-        to_mate = either(
-            both(d == 3, p == 0), both(d == 1, p == 1),
-            both(d == 2, first, p == 0), both(d == 2, jnp.logical_not(first), p == 1),
-        )
-        to_out = either(both(d == 3, p == 1, first), both(d == 1, p == 0, jnp.logical_not(first)))
-        return d, to_mate, to_out
+        from_origin = either(both(d == 3, p == 0), both(d == 1, p == 1))
+        from_mate = either(both(d == 3, p == 1), both(d == 1, p == 0))
+        return d, from_origin, from_mate
 
     def chain_copy(m, way):
         device = (mate, c) if way == 0 else (out_row, 8 * y + 2 * out_h + core)
-        return remote(piece(m, x), piece(m, x), chain_send.at[m, way], slab_recv.at[m], device)
+        return remote(piece(m, x), piece(m, x), chain_send.at[m], slab_recv.at[m], device)
 
     def wide_copy(m, o):
         return remote(piece(m, x), piece(m, x), wide_send.at[m, o - 1], wide_recv.at[m, o - 1], ((r + 2 * o) % rows, c))
@@ -172,23 +168,33 @@
         at = (x - o + rows // 2) % (rows // 2)
         return remote(piece(m, x), piece(m, at), wide_send.at[m, o - 1], wide_recv.at[m, o - 1], (mate, c))
 
-    def chain_step(m, far):
-        d, to_mate, to_out = chain_conds(m)
-
-        @pl.when((d == 2) if far else (d % 2 == 1))
+    def widen(m):
+        for o in range(1, rows // 2):
+            wide_copy(m, o).start()
+
+    def origin_step(m):
+        @pl.when(chain_conds(m)[1])
         def _():
             chain_copy(m, 0).wait_recv()
-
-            @pl.when(to_mate)
-            def _():
-                chain_copy(m, 0).start()
-
-            @pl.when(to_out)
-            def _():
-                chain_copy(m, 1).start()
-
-            for o in range(1, rows // 2):
-                wide_copy(m, o).start()
+            chain_copy(m, 0).start()
+
+    def origin_widen(m):
+        @pl.when(chain_conds(m)[1])
+        def _():
+            widen(m)
+
+    def mate_step(m):
+        @pl.when(chain_conds(m)[2])
+        def _():
+            chain_copy(m, 1).wait_recv()
+            chain_copy(m, 1).start()
+            widen(m)
+
+    def far_step(m):
+        @pl.when(far_of(m) == 2)
+        def _():
+            chain_copy(m, 0).wait_recv()
+            widen(m)
 
     row_id = lax.broadcasted_iota(jnp.int32, (8, BS), 0)
     lane_id = lax.broadcasted_iota(jnp.int32, (8, BS), 1)
@@ -242,9 +248,9 @@
         split_rows(near_at + k)
 
     each(4, halo_step)
-    each(4, lambda m: chain_step(m, False))
+    each(4, origin_step)
     each(4, lambda k: halo_step(4 + k))
-    each(4, lambda m: chain_step(m, True))
+    each(4, origin_widen)
 
     @pl.when(has_far_from)
     def _():
@@ -281,6 +287,8 @@
                 for b in range(2):
                     gs[e][8 + 2 * mine + b] = stage[e, hp, b]
         each(4, advect)
+        if e == 0:
+            each(4, mate_step)
 
     for m in range(4):
         @pl.when(base + m != c)
@@ -319,74 +327,78 @@
     def got_back(e, hp):
         return remote(res.at[e, 0], resin.at[e, hp], back_send.at[e, 0], back_recv.at[e, hp], (mate, c))
 
-    def split_pair(g, at):
+    def split_pair(e, at):
         for b in range(2):
-            high, low = halves(g[at + b])
-            gh[at + b] = high
-            gl[at + b] = low
-
-    for e in range(2):
-        def own_step(m, e=e):
-            @pl.when(base + m != c)
-            def _():
-                got_in(e, m).wait_recv()
-
-            share_copy(e, m).start()
-
-            @pl.when(has_side)
-            def _():
-                side_copy(e, m).start()
-
-            split_pair(gs[e], 8 + 2 * m)
-
-        each(4, own_step)
-
-        if e == 0:
-            to_scalars.wait()
-
-            @pl.when(local_owner)
-            def _():
-                load_a2.wait()
-
-            def slab_step(m):
-                @pl.when(both(far_of(m) == 0, base + m != c))
-                def _():
-                    remote(a2_ref, a2f.at[m], slab_send.at[0], slab_recv.at[m], (r, other)).wait_recv()
-
-                @pl.when(far_of(m) != 0)
-                def _():
-                    for o in range(1, rows // 2):
-                        got_wide(m, o).wait_recv()
-
-                for jj in range(2):
-                    for t in range(BAND):
-                        high, low = halves(a2f[m, jj, t])
-                        a2s[2 * m + jj, 0:BS, t * BS:(t + 1) * BS] = high
-                        a2s[2 * m + jj, BS:2 * BS, t * BS:(t + 1) * BS] = low
-
-            each(4, slab_step)
-
-        def neighbour_step(m, e=e):
-            got_share(e, m).wait_recv()
-            split_pair(gs[e], 16 - 16 * core + 2 * m)
-
-            @pl.when(has_side)
-            def _():
-                got_side(e, m).wait_recv()
-                split_pair(gs[e], 16 * core + 2 * m)
-
-        each(4, neighbour_step)
-
-        def second(m, e=e):
-            for jj in range(2):
-                ids = [jnp.clip(bands[m, jj, t] - 2 * base + REACH, 0, 23) for t in range(BAND)]
-                res[e, m, jj] = product(a2s[2 * m + jj], [gh[k] for k in ids], [gl[k] for k in ids])
-
-            @pl.when(base + m != c)
-            def _():
-                back_copy(e, m).start()
-
-        each(4, second)
+            high, low = halves(gs[e][at + b])
+            gh[e, at + b] = high
+            gl[e, at + b] = low
+
+    near = jnp.where(local_owner, h % 2, 1 - h % 2)
+
+    def slab_step(m):
+        @pl.when(both(far_of(m) == 0, base + m != c))
+        def _():
+            remote(a2_ref, a2f.at[m], slab_send.at[0], slab_recv.at[m], (r, other)).wait_recv()
+
+        @pl.when(far_of(m) != 0)
+        def _():
+            for o in range(1, rows // 2):
+                got_wide(m, o).wait_recv()
+
+        for jj in range(2):
+            for t in range(BAND):
+                high, low = halves(a2f[m, jj, t])
+                a2s[2 * m + jj, 0:BS, t * BS:(t + 1) * BS] = high
+                a2s[2 * m + jj, BS:2 * BS, t * BS:(t + 1) * BS] = low
+
+    def own_step(e, m):
+        @pl.when(base + m != c)
+        def _():
+            got_in(e, m).wait_recv()
+
+        share_copy(e, m).start()
+
+        @pl.when(has_side)
+        def _():
+            side_copy(e, m).start()
+
+        split_pair(e, 8 + 2 * m)
+
+    def neighbour_step(e, m):
+        got_share(e, m).wait_recv()
+        split_pair(e, 16 - 16 * core + 2 * m)
+
+        @pl.when(has_side)
+        def _():
+            got_side(e, m).wait_recv()
+            split_pair(e, 16 * core + 2 * m)
+
+    def second(e, m):
+        for jj in range(2):
+            ids = [jnp.clip(bands[m, jj, t] - 2 * base + REACH, 0, 23) for t in range(BAND)]
+            res[e, m, jj] = product(a2s[2 * m + jj], [gh[e, k] for k in ids], [gl[e, k] for k in ids])
+
+        @pl.when(base + m != c)
+        def _():
+            back_copy(e, m).start()
+
+    each(4, lambda m: own_step(0, m))
+    each(4, far_step)
+    to_scalars.wait()
+
+    @pl.when(local_owner)
+    def _():
+        load_a2.wait()
+
+    each(2, lambda b: slab_step(2 * near + b))
+    each(4, lambda m: neighbour_step(0, m))
+    each(2, lambda b: second(0, 2 * near + b))
+    each(4, lambda m: own_step(1, m))
+    each(4, lambda m: neighbour_step(1, m))
+    each(2, lambda b: second(1, 2 * near + b))
+    each(2, lambda b: slab_step(2 - 2 * near + b))
+    each(2, lambda b: second(0, 2 - 2 * near + b))
+    each(2, lambda b: second(1, 2 - 2 * near + b))
 
     for e in range(2):
         def finish(hp, e=e):
@@ -422,18 +434,18 @@
     each(8, drain_halo)
 
     def drain(m):
-        d, to_mate, to_out = chain_conds(m)
+        d, from_origin, from_mate = chain_conds(m)
+
+        @pl.when(from_origin)
+        def _():
+            chain_copy(m, 0).wait_send()
+
+        @pl.when(from_mate)
+        def _():
+            chain_copy(m, 1).wait_send()
 
         @pl.when(d != 0)
         def _():
-            @pl.when(to_mate)
-            def _():
-                chain_copy(m, 0).wait_send()
-
-            @pl.when(to_out)
-            def _():
-                chain_copy(m, 1).wait_send()
-
             for o in range(1, rows // 2):
                 wide_copy(m, o).wait_send()
 
@@ -483,15 +495,15 @@
                 pltpu.VMEM((2, 4, 2, BS, BS), f32),
                 pltpu.VMEM((24, BS, BS), f32),
                 pltpu.VMEM((24, BS, BS), f32),
-                pltpu.VMEM((24, BS, BS), bf16),
-                pltpu.VMEM((24, BS, BS), bf16),
+                pltpu.VMEM((2, 24, BS, BS), bf16),
+                pltpu.VMEM((2, 24, BS, BS), bf16),
                 pltpu.VMEM((2, 4, 2, BS, BS), f32),
                 pltpu.VMEM((2, 4, 2, BS, BS), f32),
                 pltpu.VMEM((8, BS), i32),
                 pltpu.VMEM((4, 8, BS), i32),
                 pltpu.SMEM((4, 8, BS), i32),
                 dma((8,)), dma((8,)), dma((8,)), dma((8,)),
-                dma((2,)), dma((4,)), dma((4, 2)), dma((4, 3)), dma((4, 3)),
+                dma((2,)), dma((4,)), dma((4,)), dma((4, 3)), dma((4, 3)),
                 dma((4,)), dma((4,)), dma((2, 4)), dma((2, 4)),
                 dma((2, 4)), dma((2, 4)), dma((2, 4)), dma((2, 4)),
                 dma((2, 4)), dma((2, 4)), dma((4,)),

time: 128 us -> 109 us (0.85)
  the two profiles are of different devices: /device:TPU:95 before, /device:TPU:9 now
where the time goes in v3:
time: 109 us; the launch traced here: 107 us
  Pallas kernels  105 us (96%)
  other arithmetic  2.38 us (2%)
    pallas_call x1, Pallas kernels, body(): pl.pallas_call(lambda *refs: kernel(rows, cols, *refs), out_shape=jax.Sha...  105 us
    add x1, other arithmetic, body(): return product_t + noise_cov  2.38 us

profile of v3, /device:TPU:9, one launch (start us, length us, event | category | flops | bytes accessed | tf_op | source)
XLA Modules:
  0.0 107.0 jit_solution(1735847347335086980)
XLA Ops:
  0.0 0.0 copy-start
  0.0 104.6 %forecast.1 = f32[256,1024]{1,0:T(8,128)} custom-call(s32[8,9]{1,0:T(8,128)} %refs_0_.1, s32[2,9]{1,0:T(2,128)} %refs_1_.1, f32[8,128,256]{2,1,0:T(8,128)} %bitcast.1, f32[8,9,128,128]{3,2,1,0:T(8,128)} %refs_3_.1, f32[2,9,128,128]{3,2,1,0:T(8,128)} %refs_4_.1), custom_call_target="tpu_custom_call" | custom-call | tf_op jit(solution)/shard_map/forecast/pallas_call | solution.py:482
  104.6 0.0 copy-done
  104.6 2.4 %add.3 = f32[256,1024]{1,0:T(8,128)} add(f32[256,1024]{1,0:T(8,128)} %forecast.1, f32[256,1024]{1,0:T(8,128)S(1)} %copy-done) | non-fusion elementwise | flops 262144 | bytes 3145728 | tf_op jit(solution)/shard_map/add | solution.py:516
Async XLA Ops:
  0.0 104.6 %copy-start = (f32[256,1024]{1,0:T(8,128)S(1)}, f32[256,1024]{1,0:T(8,128)}, u32[]{:S(2)}) copy-start(f32[256,1024]{1,0:T(8,128)} %param.11) | copy-start | bytes 3145732

commit v4 on v3

--- a/solution.py
+++ b/solution.py
@@ -86,11 +86,17 @@
     out_row = r + 1 - 2 * p
     out_h = (h + 3 + 2 * p) % 4
 
-    load_own = pltpu.make_async_copy(s_ref, hb.at[pl.ds(8, 8)], local_sem.at[0])
-    load_a1 = pltpu.make_async_copy(a1_ref, a1f, local_sem.at[1])
-    load_a2 = pltpu.make_async_copy(a2_ref, a2f.at[mine], local_sem.at[2])
-    load_own.start()
+    def half(b):
+        return slice(b * BS, (b + 1) * BS)
+
+    loads_own = [
+        pltpu.make_async_copy(s_ref.at[:, :, half(b)], hb.at[b, pl.ds(8, 8)], local_sem.at[b]) for b in range(2)
+    ]
+    load_a1 = pltpu.make_async_copy(a1_ref, a1f, local_sem.at[2])
+    load_a2 = pltpu.make_async_copy(a2_ref, a2f.at[mine], local_sem.at[3])
+    loads_own[0].start()
     load_a1.start()
+    loads_own[1].start()
 
     @pl.when(local_owner)
     def _():
@@ -118,19 +124,27 @@
     near_at = 16 - 16 * p
     away_at = 16 * p
 
-    def send_own(k):
-        return remote(s_ref.at[k], hb.at[16 * p + k], own_send.at[k], direct_recv.at[k], (mate, c))
-
-    def got_direct(k):
-        return remote(s_ref.at[k], hb.at[near_at + k], own_send.at[k], direct_recv.at[k], (mate, c))
-
-    def send_far(k):
-        return remote(hb.at[near_at + k], hb.at[16 * p + k], far_send.at[k], far_recv.at[k], (far_to, c))
-
-    def got_far(k):
-        return remote(hb.at[near_at + k], hb.at[away_at + k], far_send.at[k], far_recv.at[k], (mate, c))
-
-    each(8, lambda k: send_own(k).start())
+    def send_own(b, k):
+        return remote(
+            s_ref.at[pl.ds(2 * k, 2), :, half(b)], hb.at[b, pl.ds(16 * p + 2 * k, 2)],
+            own_send.at[b, k], direct_recv.at[b, k], (mate, c),
+        )
+
+    def send_far(b, k):
+        return remote(
+            hb.at[b, pl.ds(near_at + 2 * k, 2)], hb.at[b, pl.ds(16 * p + 2 * k, 2)],
+            far_send.at[b, k], far_recv.at[b, k], (far_to, c),
+        )
+
+    def got_direct(b, k):
+        at = hb.at[b, pl.ds(near_at + 2 * k, 2)]
+        return remote(at, at, own_send.at[b, k], direct_recv.at[b, k], (mate, c))
+
+    def got_far(b, k):
+        at = hb.at[b, pl.ds(away_at + 2 * k, 2)]
+        return remote(at, at, far_send.at[b, k], far_recv.at[b, k], (mate, c))
+
+    each(4, lambda k: send_own(0, k).start())
 
     part = BS // (rows // 2)
 
@@ -188,6 +202,10 @@
         def _():
             chain_copy(m, 1).wait_recv()
             chain_copy(m, 1).start()
+
+    def mate_widen(m):
+        @pl.when(chain_conds(m)[2])
+        def _():
             widen(m)
 
     def far_step(m):
@@ -225,101 +243,112 @@
         def _():
             band_copy(o).start()
 
-    load_own.wait()
+    loads_own[0].wait()
     load_a1.wait()
 
-    def split_rows(at):
-        high, low = halves(hb[at])
-        hbh[at] = high
-        hbl[at] = low
-
-    def halo_step(k):
+    def split_rows(b, at):
+        for n in range(2):
+            high, low = halves(hb[b, at + n])
+            hbh[b, at + n] = high
+            hbl[b, at + n] = low
+
+    def split_first(i):
         for t in range(BAND):
-            high, low = halves(a1f[k, t])
-            a1s[k, 0:BS, t * BS:(t + 1) * BS] = high
-            a1s[k, BS:2 * BS, t * BS:(t + 1) * BS] = low
-        split_rows(8 + k)
-        got_direct(k).wait_recv()
+            high, low = halves(a1f[i, t])
+            a1s[i, 0:BS, t * BS:(t + 1) * BS] = high
+            a1s[i, BS:2 * BS, t * BS:(t + 1) * BS] = low
+
+    def direct_step(b, k):
+        split_rows(b, 8 + 2 * k)
+        got_direct(b, k).wait_recv()
 
         @pl.when(has_far_to)
         def _():
-            send_far(k).start()
-
-        split_rows(near_at + k)
-
-    each(4, halo_step)
+            send_far(b, k).start()
+
+        split_rows(b, near_at + 2 * k)
+
+    def away_step(b, k):
+        @pl.when(has_far_from)
+        def _():
+            got_far(b, k).wait_recv()
+            split_rows(b, away_at + 2 * k)
+
+    gs = (g0, g1)
+
+    def in_copy(b, e, o):
+        hp = (h + o) % 4
+        return group_copy(
+            stage.at[e, hp, b], gs[e].at[8 + 2 * mine + b], in_send.at[b, e, o], in_recv.at[b, e, mine], o
+        )
+
+    def got_in(b, e, m):
+        at = gs[e].at[8 + 2 * m + b]
+        return remote(at, at, in_send.at[b, e, 0], in_recv.at[b, e, m], (mate, c))
+
+    def advect(b, e, n):
+        o = 3 - n
+        hp = (h + o) % 4
+        i = 2 * hp + e
+        ids = [jnp.clip(band1[i, t] - 8 * r + REACH, 0, 23) for t in range(BAND)]
+        tile = product(a1s[i], [hbh[b, k] for k in ids], [hbl[b, k] for k in ids]).T
+        stage[e, hp, b] = tile
+
+        @pl.when(is_remote(o))
+        def _():
+            in_copy(b, e, o).start()
+
+        @pl.when(jnp.logical_not(is_remote(o)))
+        def _():
+            gs[e][8 + 2 * mine + b] = tile
+
+    def first_step(k):
+        for n in range(2):
+            split_first(2 * k + n)
+        direct_step(0, k)
+
+    each(3, first_step)
     each(4, origin_step)
-    each(4, lambda k: halo_step(4 + k))
+    each(4, lambda k: send_own(1, k).start())
+    first_step(3)
     each(4, origin_widen)
-
-    @pl.when(has_far_from)
-    def _():
-        def step(k):
-            got_far(k).wait_recv()
-            split_rows(away_at + k)
-        each(8, step)
-
-    gs = (g0, g1)
-
-    def in_copy(e, o):
-        hp = (h + o) % 4
-        return group_copy(stage.at[e, hp], gs[e].at[pl.ds(8 + 2 * mine, 2)], in_send.at[e, o], in_recv.at[e, mine], o)
-
-    def got_in(e, m):
-        return remote(stage.at[e, 0], gs[e].at[pl.ds(8 + 2 * m, 2)], in_send.at[e, 0], in_recv.at[e, m], (mate, c))
-
-    for e in range(2):
-        def advect(n, e=e):
-            o = 3 - n
-            hp = (h + o) % 4
-            i = 2 * hp + e
-            ids = [jnp.clip(band1[i, t] - 8 * r + REACH, 0, 23) for t in range(BAND)]
-            tile = product(a1s[i], [hbh[k] for k in ids], [hbl[k] for k in ids])
-            for b in range(2):
-                stage[e, hp, b] = tile[:, b * BS:(b + 1) * BS].T
-
-            @pl.when(is_remote(o))
-            def _():
-                in_copy(e, o).start()
-
-            @pl.when(jnp.logical_not(is_remote(o)))
-            def _():
-                for b in range(2):
-                    gs[e][8 + 2 * mine + b] = stage[e, hp, b]
-        each(4, advect)
-        if e == 0:
-            each(4, mate_step)
+    loads_own[1].wait()
+    each(4, lambda k: away_step(0, k))
+    each(4, lambda n: advect(0, 0, n))
+    each(4, mate_step)
+    each(4, lambda n: advect(0, 1, n))
+    each(4, lambda k: direct_step(1, k))
+    each(4, mate_widen)
+    each(4, lambda k: away_step(1, k))
+    each(4, lambda n: advect(1, 0, n))
+    each(4, lambda n: advect(1, 1, n))
 
     for m in range(4):
         @pl.when(base + m != c)
         def _():
             got_band(m).wait_recv()
-    to_scalars = pltpu.make_async_copy(band_all, bands, local_sem.at[3])
+    to_scalars = pltpu.make_async_copy(band_all, bands, local_sem.at[4])
     to_scalars.start()
 
-    def share_copy(e, m):
+    def share_copy(b, e, m):
         return remote(
-            gs[e].at[pl.ds(8 + 2 * m, 2)], gs[e].at[pl.ds(16 * core + 2 * m, 2)],
-            share_send.at[e, m], share_recv.at[e, m], (r, other),
+            gs[e].at[8 + 2 * m + b], gs[e].at[16 * core + 2 * m + b],
+            share_send.at[b, e, m], share_recv.at[b, e, m], (r, other),
         )
 
-    def side_copy(e, m):
+    def side_copy(b, e, m):
         return remote(
-            gs[e].at[pl.ds(8 + 2 * m, 2)], gs[e].at[pl.ds(16 - 16 * core + 2 * m, 2)],
-            side_send.at[e, m], side_recv.at[e, m], (r, side),
+            gs[e].at[8 + 2 * m + b], gs[e].at[16 - 16 * core + 2 * m + b],
+            side_send.at[b, e, m], side_recv.at[b, e, m], (r, side),
         )
 
-    def got_share(e, m):
-        return remote(
-            gs[e].at[pl.ds(8 + 2 * m, 2)], gs[e].at[pl.ds(16 - 16 * core + 2 * m, 2)],
-            share_send.at[e, m], share_recv.at[e, m], (r, other),
-        )
-
-    def got_side(e, m):
-        return remote(
-            gs[e].at[pl.ds(8 + 2 * m, 2)], gs[e].at[pl.ds(16 * core + 2 * m, 2)],
-            side_send.at[e, m], side_recv.at[e, m], (r, other),
-        )
+    def got_share(b, e, m):
+        at = gs[e].at[16 - 16 * core + 2 * m + b]
+        return remote(at, at, share_send.at[b, e, m], share_recv.at[b, e, m], (r, other))
+
+    def got_side(b, e, m):
+        at = gs[e].at[16 * core + 2 * m + b]
+        return remote(at, at, side_send.at[b, e, m], side_recv.at[b, e, m], (r, other))
 
     def back_copy(e, m):
         return remote(res.at[e, m], resin.at[e, h], back_send.at[e, m], back_recv.at[e, h], (r, base + m))
@@ -327,11 +356,10 @@
     def got_back(e, hp):
         return remote(res.at[e, 0], resin.at[e, hp], back_send.at[e, 0], back_recv.at[e, hp], (mate, c))
 
-    def split_pair(e, at):
-        for b in range(2):
-            high, low = halves(gs[e][at + b])
-            gh[e, at + b] = high
-            gl[e, at + b] = low
+    def split_block(e, at):
+        high, low = halves(gs[e][at])
+        gh[e, at] = high
+        gl[e, at] = low
 
     near = jnp.where(local_owner, h % 2, 1 - h % 2)
 
@@ -351,27 +379,27 @@
                 a2s[2 * m + jj, 0:BS, t * BS:(t + 1) * BS] = high
                 a2s[2 * m + jj, BS:2 * BS, t * BS:(t + 1) * BS] = low
 
-    def own_step(e, m):
+    def own_step(b, e, m):
         @pl.when(base + m != c)
         def _():
-            got_in(e, m).wait_recv()
-
-        share_copy(e, m).start()
+            got_in(b, e, m).wait_recv()
+
+        share_copy(b, e, m).start()
 
         @pl.when(has_side)
         def _():
-            side_copy(e, m).start()
-
-        split_pair(e, 8 + 2 * m)
-
-    def neighbour_step(e, m):
-        got_share(e, m).wait_recv()
-        split_pair(e, 16 - 16 * core + 2 * m)
+            side_copy(b, e, m).start()
+
+        split_block(e, 8 + 2 * m + b)
+
+    def neighbour_step(b, e, m):
+        got_share(b, e, m).wait_recv()
+        split_block(e, 16 - 16 * core + 2 * m + b)
 
         @pl.when(has_side)
         def _():
-            got_side(e, m).wait_recv()
-            split_pair(e, 16 * core + 2 * m)
+            got_side(b, e, m).wait_recv()
+            split_block(e, 16 * core + 2 * m + b)
 
     def second(e, m):
         for jj in range(2):
@@ -382,7 +410,8 @@
         def _():
             back_copy(e, m).start()
 
-    each(4, lambda m: own_step(0, m))
+    for e in range(2):
+        each(4, lambda m: own_step(0, e, m))
     each(4, far_step)
     to_scalars.wait()
 
@@ -390,15 +419,16 @@
     def _():
         load_a2.wait()
 
-    each(2, lambda b: slab_step(2 * near + b))
-    each(4, lambda m: neighbour_step(0, m))
-    each(2, lambda b: second(0, 2 * near + b))
-    each(4, lambda m: own_step(1, m))
-    each(4, lambda m: neighbour_step(1, m))
-    each(2, lambda b: second(1, 2 * near + b))
-    each(2, lambda b: slab_step(2 - 2 * near + b))
-    each(2, lambda b: second(0, 2 - 2 * near + b))
-    each(2, lambda b: second(1, 2 - 2 * near + b))
+    for e in range(2):
+        each(4, lambda m: own_step(1, e, m))
+        if e == 0:
+            each(2, lambda n: slab_step(2 * near + n))
+        for b in range(2):
+            each(4, lambda m: neighbour_step(b, e, m))
+        each(2, lambda n: second(e, 2 * near + n))
+        if e == 0:
+            each(2, lambda n: slab_step(2 - 2 * near + n))
+        each(2, lambda n: second(e, 2 - 2 * near + n))
 
     for e in range(2):
         def finish(hp, e=e):
@@ -425,13 +455,14 @@
         slab_to_mate_core.wait_send()
 
     def drain_halo(k):
-        send_own(k).wait_send()
-
-        @pl.when(has_far_to)
-        def _():
-            send_far(k).wait_send()
-
-    each(8, drain_halo)
+        for b in range(2):
+            send_own(b, k).wait_send()
+
+            @pl.when(has_far_to)
+            def _():
+                send_far(b, k).wait_send()
+
+    each(4, drain_halo)
 
     def drain(m):
         d, from_origin, from_mate = chain_conds(m)
@@ -453,14 +484,16 @@
         def _():
             band_copy(m).wait_send()
             for e in range(2):
-                in_copy(e, m).wait_send()
+                for b in range(2):
+                    in_copy(b, e, m).wait_send()
 
         for e in range(2):
-            share_copy(e, m).wait_send()
-
-            @pl.when(has_side)
-            def _():
-                side_copy(e, m).wait_send()
+            for b in range(2):
+                share_copy(b, e, m).wait_send()
+
+                @pl.when(has_side)
+                def _():
+                    side_copy(b, e, m).wait_send()
 
             @pl.when(base + m != c)
             def _():
@@ -485,9 +518,9 @@
             in_specs=[smem, smem, anyspace, anyspace, anyspace],
             out_specs=pl.BlockSpec(memory_space=pltpu.VMEM),
             scratch_shapes=[
-                pltpu.VMEM((24, BS, width), f32),
-                pltpu.VMEM((24, BS, width), bf16),
-                pltpu.VMEM((24, BS, width), bf16),
+                pltpu.VMEM((2, 24, BS, BS), f32),
+                pltpu.VMEM((2, 24, BS, BS), bf16),
+                pltpu.VMEM((2, 24, BS, BS), bf16),
                 pltpu.VMEM((8, BAND, BS, BS), f32),
                 pltpu.VMEM((8, 2 * BS, BAND * BS), bf16),
                 pltpu.VMEM((4, 2, BAND, BS, BS), f32),
@@ -502,14 +535,14 @@
                 pltpu.VMEM((8, BS), i32),
                 pltpu.VMEM((4, 8, BS), i32),
                 pltpu.SMEM((4, 8, BS), i32),
-                dma((8,)), dma((8,)), dma((8,)), dma((8,)),
+                dma((2, 4)), dma((2, 4)), dma((2, 4)), dma((2, 4)),
                 dma((2,)), dma((4,)), dma((4,)), dma((4, 3)), dma((4, 3)),
-                dma((4,)), dma((4,)), dma((2, 4)), dma((2, 4)),
-                dma((2, 4)), dma((2, 4)), dma((2, 4)), dma((2, 4)),
-                dma((2, 4)), dma((2, 4)), dma((4,)),
+                dma((4,)), dma((4,)), dma((2, 2, 4)), dma((2, 2, 4)),
+                dma((2, 2, 4)), dma((2, 2, 4)), dma((2, 2, 4)), dma((2, 2, 4)),
+                dma((2, 4)), dma((2, 4)), dma((5,)),
             ],
             compiler_params=pltpu.CompilerParams(
-                collective_id=0, has_side_effects=True, vmem_limit_bytes=60 * 2**20
+                collective_id=0, has_side_effects=True, vmem_limit_bytes=52 * 2**20
             ),
             name="forecast",
         )(band_first, band_second, tiles, trans_first, trans_second)

time: 109 us -> 104 us (0.954)
  Pallas kernels: 105 us -> 99.5 us
  local copies, waits for them, and re-layouts: 0.01 us -> 1.37 us
  other arithmetic: 2.38 us -> 1.11 us
    pallas_call x1, Pallas kernels: 105 us -> 99.5 us  [body(): pl.pallas_call(lambda *refs: kernel(rows, cols, *refs), out_shape=jax.Sha...]
    unnamed x2 -> x6, local copies, waits for them, and re-layouts: 0.01 us -> 1.37 us
    add x1, other arithmetic: 2.38 us -> 1.11 us  [body(): return product_t + noise_cov]
where the time goes in v4:
time: 104 us; the launch traced here: 102 us
  Pallas kernels  99.5 us (96%)
  local copies, waits for them, and re-layouts  1.37 us (1%)
  other arithmetic  1.11 us (1%)
    pallas_call x1, Pallas kernels, body(): pl.pallas_call(lambda *refs: kernel(rows, cols, *refs), out_shape=jax.Sha...  99.5 us

profile of v4, /device:TPU:9, one launch (start us, length us, event | category | flops | bytes accessed | tf_op | source)
XLA Modules:
  0.0 102.0 jit_solution(67042724270838138)
XLA Ops:
  0.0 0.0 copy-start
  0.0 0.7 copy-done
  0.7 0.0 copy-start.1
  0.7 0.7 copy-done.1
  1.4 0.0 copy-start.2
  1.4 99.5 %forecast.1 = f32[256,1024]{1,0:T(8,128)S(1)} custom-call(s32[8,9]{1,0:T(8,128)S(1)} %copy-done, s32[2,9]{1,0:T(2,128)S(1)} %copy-done.1, f32[8,128,256]{2,1,0:T(8,128)} %bitcast.1, f32[8,9,128,128]{3,2,1,0:T(8,128)} %refs_3_.1, f32[2,9,128,128]{3,2,1,0:T(8,128)} %refs_4_.1), custom_call_target="tpu_custom_call" | custom-call | tf_op jit(solution)/shard_map/forecast/pallas_call | solution.py:515
  100.8 0.0 copy-done.2
  100.9 1.1 %add.3 = f32[256,1024]{1,0:T(8,128)} add(f32[256,1024]{1,0:T(8,128)S(1)} %forecast.1, f32[256,1024]{1,0:T(8,128)S(1)} %copy-done.2) | non-fusion elementwise | flops 262144 | bytes 3145728 | tf_op jit(solution)/shard_map/add | solution.py:549
Async XLA Ops:
  0.0 0.7 copy-start
  0.7 0.7 copy-start.1
  1.4 99.5 %copy-start.2 = (f32[256,1024]{1,0:T(8,128)S(1)}, f32[256,1024]{1,0:T(8,128)}, u32[]{:S(2)}) copy-start(f32[256,1024]{1,0:T(8,128)} %param.11) | copy-start | bytes 3145732

commit v5 on v4

--- a/solution.py
+++ b/solution.py
@@ -182,9 +182,27 @@
         at = (x - o + rows // 2) % (rows // 2)
         return remote(piece(m, x), piece(m, at), wide_send.at[m, o - 1], wide_recv.at[m, o - 1], (mate, c))
 
+    def relay_copy(m):
+        odd = m % 2
+        at = (x + 3 - 2 * odd) % 4
+        return remote(
+            piece(m, at), piece(m, at), wide_send.at[m, 1], wide_recv.at[m, 1], ((r + 2 - 4 * odd + rows) % rows, c)
+        )
+
     def widen(m):
-        for o in range(1, rows // 2):
+        for o in (1, 3):
             wide_copy(m, o).start()
+
+    def relay(m):
+        got_wide(m, 1 + 2 * (m % 2)).wait_recv()
+        relay_copy(m).start()
+
+    def relay_step(m, kind):
+        cond = far_of(m) == 2 if kind == 0 else chain_conds(m)[kind]
+
+        @pl.when(cond)
+        def _():
+            relay(m)
 
     def origin_step(m):
         @pl.when(chain_conds(m)[1])
@@ -318,6 +336,7 @@
     each(4, mate_step)
     each(4, lambda n: advect(0, 1, n))
     each(4, lambda k: direct_step(1, k))
+    each(4, lambda m: relay_step(m, 1))
     each(4, mate_widen)
     each(4, lambda k: away_step(1, k))
     each(4, lambda n: advect(1, 0, n))
@@ -370,8 +389,8 @@
 
         @pl.when(far_of(m) != 0)
         def _():
-            for o in range(1, rows // 2):
-                got_wide(m, o).wait_recv()
+            got_wide(m, 3 - 2 * (m % 2)).wait_recv()
+            got_wide(m, 2).wait_recv()
 
         for jj in range(2):
             for t in range(BAND):
@@ -410,25 +429,29 @@
         def _():
             back_copy(e, m).start()
 
+    each(4, far_step)
+    each(4, lambda m: relay_step(m, 2))
     for e in range(2):
         each(4, lambda m: own_step(0, e, m))
-    each(4, far_step)
     to_scalars.wait()
 
     @pl.when(local_owner)
     def _():
         load_a2.wait()
 
-    for e in range(2):
-        each(4, lambda m: own_step(1, e, m))
-        if e == 0:
-            each(2, lambda n: slab_step(2 * near + n))
-        for b in range(2):
-            each(4, lambda m: neighbour_step(b, e, m))
-        each(2, lambda n: second(e, 2 * near + n))
-        if e == 0:
-            each(2, lambda n: slab_step(2 - 2 * near + n))
-        each(2, lambda n: second(e, 2 - 2 * near + n))
+    each(4, lambda m: own_step(1, 0, m))
+    each(4, lambda m: relay_step(m, 0))
+    each(2, lambda n: slab_step(2 * near + n))
+    for b in range(2):
+        each(4, lambda m: neighbour_step(b, 0, m))
+    each(2, lambda n: second(0, 2 * near + n))
+    each(4, lambda m: own_step(1, 1, m))
+    each(2, lambda n: slab_step(2 - 2 * near + n))
+    each(2, lambda n: second(0, 2 - 2 * near + n))
+    for b in range(2):
+        each(4, lambda m: neighbour_step(b, 1, m))
+    each(2, lambda n: second(1, 2 * near + n))
+    each(2, lambda n: second(1, 2 - 2 * near + n))
 
     for e in range(2):
         def finish(hp, e=e):
@@ -477,8 +500,9 @@
 
         @pl.when(d != 0)
         def _():
-            for o in range(1, rows // 2):
+            for o in (1, 3):
                 wide_copy(m, o).wait_send()
+            relay_copy(m).wait_send()
 
         @pl.when(is_remote(m))
         def _():

time: 104 us -> 101 us (0.971)
  the two profiles are of different devices: /device:TPU:9 before, /device:TPU:57 now
where the time goes in v5:
time: 101 us; the launch traced here: 100 us
  Pallas kernels  98 us (97%)
  local copies, waits for them, and re-layouts  1.37 us (1%)
  other arithmetic  1.11 us (1%)
    pallas_call x1, Pallas kernels, body(): pl.pallas_call(lambda *refs: kernel(rows, cols, *refs), out_shape=jax.Sha...  98 us

profile of v5, /device:TPU:57, one launch (start us, length us, event | category | flops | bytes accessed | tf_op | source)
XLA Modules:
  0.0 100.5 jit_solution(6834056810309228192)
XLA Ops:
  0.0 0.0 copy-start
  0.0 0.7 copy-done
  0.7 0.0 copy-start.1
  0.7 0.7 copy-done.1
  1.4 0.0 copy-start.2
  1.4 98.0 %forecast.1 = f32[256,1024]{1,0:T(8,128)S(1)} custom-call(s32[8,9]{1,0:T(8,128)S(1)} %copy-done, s32[2,9]{1,0:T(2,128)S(1)} %copy-done.1, f32[8,128,256]{2,1,0:T(8,128)} %bitcast.1, f32[8,9,128,128]{3,2,1,0:T(8,128)} %refs_3_.1, f32[2,9,128,128]{3,2,1,0:T(8,128)} %refs_4_.1), custom_call_target="tpu_custom_call" | custom-call | tf_op jit(solution)/shard_map/forecast/pallas_call | solution.py:539
  99.4 0.0 copy-done.2
  99.4 1.1 %add.3 = f32[256,1024]{1,0:T(8,128)} add(f32[256,1024]{1,0:T(8,128)S(1)} %forecast.1, f32[256,1024]{1,0:T(8,128)S(1)} %copy-done.2) | non-fusion elementwise | flops 262144 | bytes 3145728 | tf_op jit(solution)/shard_map/add | solution.py:573
Async XLA Ops:
  0.0 0.7 copy-start
  0.7 0.7 copy-start.1
  1.4 98.0 %copy-start.2 = (f32[256,1024]{1,0:T(8,128)S(1)}, f32[256,1024]{1,0:T(8,128)}, u32[]{:S(2)}) copy-start(f32[256,1024]{1,0:T(8,128)} %param.11) | copy-start | bytes 3145732

commit v6 on v5

--- a/solution.py
+++ b/solution.py
@@ -332,14 +332,15 @@
     each(4, origin_widen)
     loads_own[1].wait()
     each(4, lambda k: away_step(0, k))
+    each(4, mate_step)
     each(4, lambda n: advect(0, 0, n))
-    each(4, mate_step)
     each(4, lambda n: advect(0, 1, n))
     each(4, lambda k: direct_step(1, k))
+    each(4, mate_widen)
     each(4, lambda m: relay_step(m, 1))
-    each(4, mate_widen)
     each(4, lambda k: away_step(1, k))
     each(4, lambda n: advect(1, 0, n))
+    each(4, far_step)
     each(4, lambda n: advect(1, 1, n))
 
     for m in range(4):
@@ -429,7 +430,6 @@
         def _():
             back_copy(e, m).start()
 
-    each(4, far_step)
     each(4, lambda m: relay_step(m, 2))
     for e in range(2):
         each(4, lambda m: own_step(0, e, m))

time: 101 us -> 99.7 us (0.987)
  the two profiles are of different devices: /device:TPU:57 before, /device:TPU:9 now
where the time goes in v6:
time: 99.7 us; the launch traced here: 99.6 us
  Pallas kernels  97.1 us (97%)
  local copies, waits for them, and re-layouts  1.37 us (1%)
  other arithmetic  1.11 us (1%)
    pallas_call x1, Pallas kernels, body(): pl.pallas_call(lambda *refs: kernel(rows, cols, *refs), out_shape=jax.Sha...  97.1 us

profile of v6, /device:TPU:9, one launch (start us, length us, event | category | flops | bytes accessed | tf_op | source)
XLA Modules:
  0.0 99.6 jit_solution(6610570301411215487)
XLA Ops:
  0.0 0.0 copy-start
  0.0 0.7 copy-done
  0.7 0.0 copy-start.1
  0.7 0.7 copy-done.1
  1.4 0.0 copy-start.2
  1.4 97.1 %forecast.1 = f32[256,1024]{1,0:T(8,128)S(1)} custom-call(s32[8,9]{1,0:T(8,128)S(1)} %copy-done, s32[2,9]{1,0:T(2,128)S(1)} %copy-done.1, f32[8,128,256]{2,1,0:T(8,128)} %bitcast.1, f32[8,9,128,128]{3,2,1,0:T(8,128)} %refs_3_.1, f32[2,9,128,128]{3,2,1,0:T(8,128)} %refs_4_.1), custom_call_target="tpu_custom_call" | custom-call | tf_op jit(solution)/shard_map/forecast/pallas_call | solution.py:539
  98.5 0.0 copy-done.2
  98.5 1.1 %add.3 = f32[256,1024]{1,0:T(8,128)} add(f32[256,1024]{1,0:T(8,128)S(1)} %forecast.1, f32[256,1024]{1,0:T(8,128)S(1)} %copy-done.2) | non-fusion elementwise | flops 262144 | bytes 3145728 | tf_op jit(solution)/shard_map/add | solution.py:573
Async XLA Ops:
  0.0 0.7 copy-start
  0.7 0.7 copy-start.1
  1.4 97.1 %copy-start.2 = (f32[256,1024]{1,0:T(8,128)S(1)}, f32[256,1024]{1,0:T(8,128)}, u32[]{:S(2)}) copy-start(f32[256,1024]{1,0:T(8,128)} %param.11) | copy-start | bytes 3145732

commit v7 on v6

--- a/solution.py
+++ b/solution.py
@@ -450,8 +450,8 @@
     each(2, lambda n: second(0, 2 - 2 * near + n))
     for b in range(2):
         each(4, lambda m: neighbour_step(b, 1, m))
+    each(2, lambda n: second(1, 2 - 2 * near + n))
     each(2, lambda n: second(1, 2 * near + n))
-    each(2, lambda n: second(1, 2 - 2 * near + n))
 
     for e in range(2):
         def finish(hp, e=e):

time: 99.7 us -> 98.7 us (0.990); the launches traced: 99.6 us -> 97.2 us
  Pallas kernels: 97.1 us -> 94.7 us
    pallas_call x1, Pallas kernels: 97.1 us -> 94.7 us  [body(): pl.pallas_call(lambda *refs: kernel(rows, cols, *refs), out_shape=jax.Sha...]
where the time goes in v7:
time: 98.7 us; the launch traced here: 97.2 us
  Pallas kernels  94.7 us (96%)
  local copies, waits for them, and re-layouts  1.37 us (1%)
  other arithmetic  1.11 us (1%)
    pallas_call x1, Pallas kernels, body(): pl.pallas_call(lambda *refs: kernel(rows, cols, *refs), out_shape=jax.Sha...  94.7 us

profile of v7, /device:TPU:9, one launch (start us, length us, event | category | flops | bytes accessed | tf_op | source)
XLA Modules:
  0.0 97.2 jit_solution(13576076884408664354)
XLA Ops:
  0.0 0.0 copy-start
  0.0 0.7 copy-done
  0.7 0.0 copy-start.1
  0.7 0.7 copy-done.1
  1.4 0.0 copy-start.2
  1.4 94.7 %forecast.1 = f32[256,1024]{1,0:T(8,128)S(1)} custom-call(s32[8,9]{1,0:T(8,128)S(1)} %copy-done, s32[2,9]{1,0:T(2,128)S(1)} %copy-done.1, f32[8,128,256]{2,1,0:T(8,128)} %bitcast.1, f32[8,9,128,128]{3,2,1,0:T(8,128)} %refs_3_.1, f32[2,9,128,128]{3,2,1,0:T(8,128)} %refs_4_.1), custom_call_target="tpu_custom_call" | custom-call | tf_op jit(solution)/shard_map/forecast/pallas_call | solution.py:539
  96.1 0.0 copy-done.2
  96.1 1.1 %add.3 = f32[256,1024]{1,0:T(8,128)} add(f32[256,1024]{1,0:T(8,128)S(1)} %forecast.1, f32[256,1024]{1,0:T(8,128)S(1)} %copy-done.2) | non-fusion elementwise | flops 262144 | bytes 3145728 | tf_op jit(solution)/shard_map/add | solution.py:573
Async XLA Ops:
  0.0 0.7 copy-start
  0.7 0.7 copy-start.1
  1.4 94.7 %copy-start.2 = (f32[256,1024]{1,0:T(8,128)S(1)}, f32[256,1024]{1,0:T(8,128)}, u32[]{:S(2)}) copy-start(f32[256,1024]{1,0:T(8,128)} %param.11) | copy-start | bytes 3145732
